TPU v7x, 32 devices: a whole 2x2x4 slice. The times are simulated.
32 devices in a mesh: dp: 4 (over y, x), sp: 8 (over z, core).
Axes of the slice: x: 2, y: 2, z: 4, core: 2. Of those that a mesh axis runs over, the one named last changes fastest.
Arguments:
- tokens: bfloat16 [32768, 1024], P(('dp', 'sp')), may hold values from -6 to 6
- doc_ids: int32 [4, 8192], P('dp'), may hold values from 0 to 15, never falling along the last dimension, each value on 1 to 4096 neighbouring positions
- gain_attn: bfloat16 [1024], P('sp'), may hold values from 0.5 to 1.5
- w_query: bfloat16 [1024, 256], P('sp'), may hold values from -0.1875 to 0.1875
- w_key: bfloat16 [1024, 256], P('sp'), may hold values from -0.1875 to 0.1875
- w_value: bfloat16 [1024, 1024], P('sp'), may hold values from -0.1875 to 0.1875
- w_out: bfloat16 [1024, 1024], P(None, 'sp'), may hold values from -2 to 2
- gain_mlp: bfloat16 [1024], P('sp'), may hold values from 0.5 to 1.5
- w_gate: bfloat16 [1024, 2752], P('sp'), may hold values from -0.1875 to 0.1875
- w_up: bfloat16 [1024, 2752], P('sp'), may hold values from -0.1875 to 0.1875
- w_down: bfloat16 [2752, 1024], P(None, 'sp'), may hold values from -0.109375 to 0.109375
- cotangent: bfloat16 [32768, 1024], P(('dp', 'sp')), may hold values from -6 to 6
Outputs:
- output: bfloat16 [32768, 1024], P(('dp', 'sp'))
- grad_input: float32 [32768, 1024], P(('dp', 'sp'))
- grad_gain_attn: float32 [1024], P('sp')
- grad_query: float32 [1024, 256], P('sp')
- grad_key: float32 [1024, 256], P('sp')
- grad_value: float32 [1024, 1024], P('sp')
- grad_out: float32 [1024, 1024], P(None, 'sp')
- grad_gain_mlp: float32 [1024], P('sp')
- grad_gate: float32 [1024, 2752], P('sp')
- grad_up: float32 [1024, 2752], P('sp')
- grad_down: float32 [2752, 1024], P(None, 'sp')
Inputs may be any that keep to these rules, and one draw needn't show every extreme that they name: `doc_ids`: within each group document numbers never fall along the tokens, every number 0 to 15 is used, each document has 1 to 4096 tokens and one has exactly 4096.
All inputs are finite; a program needn't handle non-finite values.
Results may differ from a plain program's by a relative error of at most 0.019.
Values may be sent and summed in bfloat16 or wider, within the bound.
A program may use at most 192 MiB of HBM per device.

v0:
```python
import math
import jax
import jax.numpy as jnp
from jax import lax
from jax.sharding import PartitionSpec as P

FEAT = 16
HEAD_V = 64
BLOCK = 512
EPSILON = 1e-05
CAREFUL = lax.Precision.HIGH


def rms_scale(values, weights):
    return values * lax.rsqrt(jnp.mean(values * values, axis=-1, keepdims=True) + EPSILON) * weights


def taylor(vectors):
    feature_dim = vectors.shape[-1]
    scale_one = 1.0 / math.sqrt(math.sqrt(feature_dim))
    scale_two = 1.0 / (math.sqrt(2.0) * math.sqrt(feature_dim))
    products = (vectors[..., :, None] * vectors[..., None, :]).reshape(
        vectors.shape[:-1] + (feature_dim * feature_dim,)
    )
    return jnp.concatenate(
        [
            jnp.ones(vectors.shape[:-1] + (1,), vectors.dtype),
            vectors * scale_one,
            products * scale_two,
        ],
        axis=-1,
    )


def attend_block(carried, blocks):
    kv_state, key_total, last_doc = carried
    query_blk, key_blk, value_blk, doc_blk = blocks
    feature_dim = query_blk.shape[-1]
    length_blk = doc_blk.shape[0]
    scores = jnp.einsum("hif,hjf->hij", query_blk, key_blk, precision=CAREFUL)
    position = lax.iota(jnp.int32, length_blk)
    allowed = (position[:, None] >= position[None, :]) & (doc_blk[:, None] == doc_blk[None, :])
    weights = jnp.where(
        allowed[None],
        1.0 + scores / math.sqrt(feature_dim) + scores * scores / (2.0 * feature_dim),
        0.0,
    )
    query_map = taylor(query_blk)
    key_map = taylor(key_blk)
    sees_prior = (doc_blk == last_doc).astype(query_blk.dtype)
    numerator = jnp.einsum("hij,hjv->hiv", weights, value_blk, precision=CAREFUL) + sees_prior[
        None, :, None
    ] * jnp.einsum("hif,hfv->hiv", query_map, kv_state, precision=CAREFUL)
    denominator = jnp.sum(weights, axis=-1) + sees_prior[None, :] * jnp.einsum(
        "hif,hf->hi", query_map, key_total, precision=CAREFUL
    )
    attended = numerator / denominator[..., None]
    tail_doc = doc_blk[length_blk - 1]
    keep_old = (tail_doc == last_doc).astype(query_blk.dtype)
    in_tail = (doc_blk == tail_doc).astype(query_blk.dtype)
    key_tail = key_map * in_tail[None, :, None]
    kv_state = keep_old * kv_state + jnp.einsum(
        "hjf,hjv->hfv", key_tail, value_blk, precision=CAREFUL
    )
    key_total = keep_old * key_total + jnp.sum(key_tail, axis=1)
    return ((kv_state, key_total, tail_doc), attended)


def attend(queries, keys_in, values_in, doc_row):
    head_count, feature_dim, length = queries.shape
    value_dim = values_in.shape[1]
    block_count = length // BLOCK
    mapped_dim = 1 + feature_dim + feature_dim * feature_dim

    def blocked(tensor):
        inner_dim = tensor.shape[1]
        return tensor.reshape(head_count, inner_dim, block_count, BLOCK).transpose(2, 0, 3, 1)

    initial = (
        jnp.zeros((head_count, mapped_dim, value_dim), queries.dtype),
        jnp.zeros((head_count, mapped_dim), queries.dtype),
        jnp.array(-1, jnp.int32),
    )
    _, outputs = lax.scan(
        jax.checkpoint(attend_block),
        initial,
        (
            blocked(queries),
            blocked(keys_in),
            blocked(values_in),
            doc_row.reshape(block_count, BLOCK),
        ),
    )
    return outputs.transpose(1, 3, 0, 2).reshape(head_count, value_dim, length)


def joined(query_w, key_w, value_w):
    model_dim = query_w.shape[0]
    head_count = query_w.shape[1] // FEAT
    stacked = jnp.concatenate(
        [
            query_w.reshape(model_dim, head_count, FEAT),
            key_w.reshape(model_dim, head_count, FEAT),
            value_w.reshape(model_dim, head_count, HEAD_V),
        ],
        axis=2,
    )
    return stacked.reshape(model_dim, head_count * (2 * FEAT + HEAD_V))


def body(
    tokens,
    doc_ids,
    gain_attn,
    w_query,
    w_key,
    w_value,
    w_out,
    gain_mlp,
    w_gate,
    w_up,
    w_down,
    cotangent,
):
    head_count = w_query.shape[1] // FEAT
    shard_sp = lax.axis_size("sp")
    heads_here = head_count // shard_sp
    per_head = 2 * FEAT + HEAD_V
    tok_local = tokens.shape[0]
    contract_first = (((0,), (0,)), ((), ()))
    attn_full = (
        lax.all_gather(gain_attn, "sp", axis=0, tiled=True),
        lax.all_gather(w_query, "sp", axis=0, tiled=True),
        lax.all_gather(w_key, "sp", axis=0, tiled=True),
        lax.all_gather(w_value, "sp", axis=0, tiled=True),
        lax.all_gather(w_out, "sp", axis=1, tiled=True),
    )
    mlp_full = (
        lax.all_gather(gain_mlp, "sp", axis=0, tiled=True),
        lax.all_gather(w_gate, "sp", axis=0, tiled=True),
        lax.all_gather(w_up, "sp", axis=0, tiled=True),
        lax.all_gather(w_down, "sp", axis=1, tiled=True),
    )
    resid = tokens.astype(jnp.float32)
    gain_one = attn_full[0].astype(jnp.float32)
    w_joint = joined(attn_full[1], attn_full[2], attn_full[3])
    model_dim = w_joint.shape[0]
    normed_one = rms_scale(resid, gain_one).astype(jnp.bfloat16)
    projected = lax.dot_general(
        w_joint, normed_one, (((0,), (1,)), ((), ())), preferred_element_type=jnp.float32
    ).astype(jnp.bfloat16)
    by_head = lax.all_to_all(
        projected.reshape(head_count, per_head, tok_local),
        "sp",
        split_axis=0,
        concat_axis=2,
        tiled=True,
    )
    head_rows = by_head.astype(jnp.float32)
    doc_row = doc_ids[0]

    def local_attention(queries, keys_in, values_in):
        return attend(queries, keys_in, values_in, doc_row)

    attended, attention_back = jax.vjp(
        local_attention,
        head_rows[:, :FEAT],
        head_rows[:, FEAT : 2 * FEAT],
        head_rows[:, 2 * FEAT :],
    )
    attended_rows = attended.astype(jnp.bfloat16).reshape(heads_here * HEAD_V, attended.shape[2])
    token_heads = lax.all_to_all(attended_rows, "sp", split_axis=1, concat_axis=0, tiled=True)
    branch = lax.dot_general(
        token_heads, attn_full[4], contract_first, preferred_element_type=jnp.float32
    )
    hidden = resid + branch
    gain_two = mlp_full[0].astype(jnp.float32)
    normed_two = rms_scale(hidden, gain_two).astype(jnp.bfloat16)
    gate = jnp.dot(normed_two, mlp_full[1], preferred_element_type=jnp.float32)
    up_proj = jnp.dot(normed_two, mlp_full[2], preferred_element_type=jnp.float32)
    sigmoid_gate = jax.nn.sigmoid(gate)
    mixed = (gate * sigmoid_gate * up_proj).astype(jnp.bfloat16)
    output = (hidden + jnp.dot(mixed, mlp_full[3], preferred_element_type=jnp.float32)).astype(
        jnp.bfloat16
    )
    fetched = (
        lax.all_gather(gain_attn, "sp", axis=0, tiled=True),
        lax.all_gather(w_query, "sp", axis=0, tiled=True),
        lax.all_gather(w_key, "sp", axis=0, tiled=True),
        lax.all_gather(w_value, "sp", axis=0, tiled=True),
        lax.all_gather(w_out, "sp", axis=1, tiled=True),
        lax.all_gather(gain_mlp, "sp", axis=0, tiled=True),
        lax.all_gather(w_gate, "sp", axis=0, tiled=True),
        lax.all_gather(w_up, "sp", axis=0, tiled=True),
        lax.all_gather(w_down, "sp", axis=1, tiled=True),
    )
    out_back = fetched[4]
    gate_back = fetched[6]
    up_back = fetched[7]
    down_back = fetched[8]
    joint_back = joined(fetched[1], fetched[2], fetched[3])
    grad_top = cotangent.astype(jnp.float32)
    grad_down = lax.dot_general(
        mixed, cotangent, contract_first, preferred_element_type=jnp.float32
    )
    grad_mixed = lax.dot_general(
        cotangent, down_back, (((1,), (1,)), ((), ())), preferred_element_type=jnp.float32
    )
    grad_gate_in = (
        grad_mixed * up_proj * sigmoid_gate * (1.0 + gate * (1.0 - sigmoid_gate))
    ).astype(jnp.bfloat16)
    grad_up_in = (grad_mixed * gate * sigmoid_gate).astype(jnp.bfloat16)
    grad_gate = lax.dot_general(
        normed_two, grad_gate_in, contract_first, preferred_element_type=jnp.float32
    )
    grad_up = lax.dot_general(
        normed_two, grad_up_in, contract_first, preferred_element_type=jnp.float32
    )
    grad_normed_two = lax.dot_general(
        grad_gate_in, gate_back, (((1,), (1,)), ((), ())), preferred_element_type=jnp.float32
    ) + lax.dot_general(
        grad_up_in, up_back, (((1,), (1,)), ((), ())), preferred_element_type=jnp.float32
    )
    _, norm_two_back = jax.vjp(rms_scale, hidden, gain_two)
    grad_hidden_part, grad_gain_two = norm_two_back(grad_normed_two)
    grad_hidden = grad_top + grad_hidden_part
    grad_branch = grad_hidden.astype(jnp.bfloat16)
    grad_out = jnp.dot(token_heads, grad_branch, preferred_element_type=jnp.float32)
    grad_attended = lax.dot_general(
        out_back, grad_branch, (((1,), (1,)), ((), ())), preferred_element_type=jnp.float32
    ).astype(jnp.bfloat16)
    grad_heads = lax.all_to_all(grad_attended, "sp", split_axis=0, concat_axis=1, tiled=True)
    grad_q, grad_k, grad_v = attention_back(
        grad_heads.astype(jnp.float32).reshape(heads_here, HEAD_V, grad_heads.shape[1])
    )
    grad_stack = jnp.concatenate([grad_q, grad_k, grad_v], axis=1).astype(jnp.bfloat16)
    grad_proj = lax.all_to_all(grad_stack, "sp", split_axis=2, concat_axis=0, tiled=True).reshape(
        head_count * per_head, tok_local
    )
    grad_joint = lax.dot_general(
        normed_one, grad_proj, (((0,), (1,)), ((), ())), preferred_element_type=jnp.float32
    ).reshape(model_dim, head_count, per_head)
    grad_query = grad_joint[:, :, :FEAT].reshape(model_dim, head_count * FEAT)
    grad_key = grad_joint[:, :, FEAT : 2 * FEAT].reshape(model_dim, head_count * FEAT)
    grad_value = grad_joint[:, :, 2 * FEAT :].reshape(model_dim, head_count * HEAD_V)
    grad_normed_one = lax.dot_general(
        grad_proj, joint_back, (((0,), (1,)), ((), ())), preferred_element_type=jnp.float32
    )
    _, norm_one_back = jax.vjp(rms_scale, resid, gain_one)
    grad_input_part, grad_gain_one = norm_one_back(grad_normed_one)
    grad_input = grad_hidden + grad_input_part
    shards = (
        lax.psum_scatter(
            grad_gain_one.astype(jnp.bfloat16), "sp", scatter_dimension=0, tiled=True
        ).astype(jnp.float32),
        lax.psum_scatter(
            grad_query.astype(jnp.bfloat16), "sp", scatter_dimension=0, tiled=True
        ).astype(jnp.float32),
        lax.psum_scatter(
            grad_key.astype(jnp.bfloat16), "sp", scatter_dimension=0, tiled=True
        ).astype(jnp.float32),
        lax.psum_scatter(
            grad_value.astype(jnp.bfloat16), "sp", scatter_dimension=0, tiled=True
        ).astype(jnp.float32),
        lax.psum_scatter(
            grad_out.astype(jnp.bfloat16), "sp", scatter_dimension=1, tiled=True
        ).astype(jnp.float32),
        lax.psum_scatter(
            grad_gain_two.astype(jnp.bfloat16), "sp", scatter_dimension=0, tiled=True
        ).astype(jnp.float32),
        lax.psum_scatter(
            grad_gate.astype(jnp.bfloat16), "sp", scatter_dimension=0, tiled=True
        ).astype(jnp.float32),
        lax.psum_scatter(
            grad_up.astype(jnp.bfloat16), "sp", scatter_dimension=0, tiled=True
        ).astype(jnp.float32),
        lax.psum_scatter(
            grad_down.astype(jnp.bfloat16), "sp", scatter_dimension=1, tiled=True
        ).astype(jnp.float32),
    )
    summed = (
        lax.psum(shards[0].astype(jnp.bfloat16), "dp").astype(jnp.float32),
        lax.psum(shards[1].astype(jnp.bfloat16), "dp").astype(jnp.float32),
        lax.psum(shards[2].astype(jnp.bfloat16), "dp").astype(jnp.float32),
        lax.psum(shards[3].astype(jnp.bfloat16), "dp").astype(jnp.float32),
        lax.psum(shards[4].astype(jnp.bfloat16), "dp").astype(jnp.float32),
        lax.psum(shards[5].astype(jnp.bfloat16), "dp").astype(jnp.float32),
        lax.psum(shards[6].astype(jnp.bfloat16), "dp").astype(jnp.float32),
        lax.psum(shards[7].astype(jnp.bfloat16), "dp").astype(jnp.float32),
        lax.psum(shards[8].astype(jnp.bfloat16), "dp").astype(jnp.float32),
    )
    return (
        output,
        grad_input,
        summed[0],
        summed[1],
        summed[2],
        summed[3],
        summed[4],
        summed[5],
        summed[6],
        summed[7],
        summed[8],
    )


def solution(mesh):
    placed = (
        P(("dp", "sp"), None),
        P("dp", None),
        P("sp"),
        P("sp", None),
        P("sp", None),
        P("sp", None),
        P(None, "sp"),
        P("sp"),
        P("sp", None),
        P("sp", None),
        P(None, "sp"),
        P(("dp", "sp"), None),
    )
    return jax.shard_map(
        body,
        mesh=mesh,
        in_specs=placed,
        out_specs=(
            P(("dp", "sp"), None),
            P(("dp", "sp"), None),
            P("sp"),
            P("sp", None),
            P("sp", None),
            P("sp", None),
            P(None, "sp"),
            P("sp"),
            P("sp", None),
            P("sp", None),
            P(None, "sp"),
        ),
        check_vma=False,
    )
```

profile of v0, /device:TPU:0, one launch (start us, length us, event | category | flops | bytes accessed | tf_op | source)
XLA Modules:
  0.0 1510.6 jit_solution(1957601974484054943)
XLA Ops:
  14.1 13.4 all-gather
  28.8 16.1 %all_gather.34 = bf16[1024,256]{0,1:T(8,128)(2,1)S(1)} all-gather(bf16[128,256]{0,1:T(8,128)(2,1)S(1)} %copy.123), channel_id=1, replica_groups=mesh['dp'=4,'sp'=8] {'sp'}, dimensions={0}, use_global_device_ids=true | all-gather | bytes 589824 | tf_op jit(solution)/shard_map/all_gather | solution.py:133
  45.0 13.9 all_gather.35
  60.9 5.0 convolution_convert_fusion.3
  65.9 4.6 all-to-all-start
  73.0 115.9 %all-to-all-done = bf16[16,96,1024]{2,1,0:T(8,128)(2,1)} async-done(((bf16[16,96,1024]{2,1,0:T(8,128)(2,1)}), bf16[16,96,1024]{2,1,0:T(8,128)(2,1)}, u32[]{:S(2)}, u32[]{:S(2)}) %all-to-all-start) | async-done | bytes 3145760 | tf_op jit(solution)/shard_map/all_to_all | solution.py:152
  201.8 4.4 copy.128
  207.8 278.0 %while.47 = (s32[]{:T(128)}, f32[2,273,64]{1,2,0:T(8,128)S(1)}, f32[2,273]{1,0:T(2,128)S(1)}, s32[]{:T(128)}, bf16[16,2,512,64]{2,3,1,0:T(8,128)(2,1)}, /*index=...) while((s32[]{:T(128)}, f32[2,273,64]{1,2,0:T(8,128)S(1)}, ...), condition=%wide.region_4.5_spmd.clone, body=%wide.region_1.4_spmd.clone.sunk | while | flops 477021408 | bytes 14363353 | solution.py:84
  485.8 4.2 copy.130
  490.0 4.1 convert_element_type.212
  494.1 4.2 copy.131
  498.2 5.5 all-to-all-start.1
  503.8 41.4 %all-gather.1 = bf16[8,1,128]{2,1,0:T(2,128)(2,1)S(1)} all-gather(bf16[1,1,128]{2,1,0:T(2,128)(2,1)S(1)} %bitcast.362), channel_id=1, replica_groups=mesh['dp'=4,'sp'=8] {'sp'}, dimensions={0}, use_global_device_ids=true | all-gather | bytes 2304 | tf_op jit(solution)/shard_map/all_gather | solution.py:139
  545.2 4.4 copy.133
  553.0 4.8 multiply_reduce_fusion.6
  561.5 11.3 fusion.89
  572.8 11.3 fusion.88
  584.1 20.1 %multiply_convert_fusion = (bf16[1024,2752]{0,1:T(8,128)(2,1)}, bf16[1024,2752]{0,1:T(8,128)(2,1)}, bf16[1024,2752]{0,1:T(8,128)(2,1)}) fusion(f32[1024,2752]{0,1:T(8,128)} %fusion.88, f32[1024,2752]{0,1:T(8,128)} %fusion.89, bf16[1024,1024]{1,0:T(8,128)(2,1)S(1)} %copy-done.9, bf16[2752,1024]{1,0:T(8,128)(2,1)} %all-gather.16.cloned.1.call-done), kind=kOutput, calls=%fused_computation.130 | convolution fusion | flops 5816451072 | bytes 47185920 | tf_op jit(solution)/shard_map/dot_general | solution.py:206
  604.2 11.5 fusion.87
  615.7 10.2 multiply_reduce_fusion.4
  629.0 5.3 convolution_convert_fusion.6
  638.3 10.8 convolution_convert_fusion
  649.1 8.3 copy.183
  659.1 10.5 convolution_convert_fusion.2
  669.6 8.3 copy.179
  679.5 5.9 convolution_convert_fusion.5
  685.3 10.1 all-to-all-start.2
  695.6 10.3 convolution_convert_fusion.1
  705.8 8.4 copy.181
  714.3 64.4 %all-to-all-done.2 = bf16[8,128,1024]{2,1,0:T(8,128)(2,1)S(1)} async-done(((bf16[8,128,1024]{2,1,0:T(8,128)(2,1)}), bf16[8,128,1024]{2,1,0:T(8,128)(2,1)S(1)}, u32[]{:S(2)}, u32[]{:S(2)}) %all-to-all-start.2) | async-done | bytes 2097184 | tf_op jit(solution)/shard_map/all_to_all | solution.py:232
  779.2 4.4 copy.136
  783.6 5.0 reshape.355
  790.2 394.0 %while.48 = (s32[]{:T(128)}, f32[2,273,64]{1,2,0:T(8,128)S(1)}, f32[2,273]{1,0:T(2,128)S(1)}, bf16[16,2,512,16]{2,3,1,0:T(8,128)(2,1)S(1)}, bf16[16,2,512,16]{2,...) while((s32[]{:T(128)}, f32[2,273,64]{1,2,0:T(8,128)S(1)}, ...), condition=%wide.region_14.15_spmd.clone, body=%wide.region_7.14_spmd.clone.sunk | while | flops 1318872064 | bytes 42693776 | solution.py:84
  1186.3 7.0 copy.144
  1193.3 98.5 %all_to_all.53 = bf16[2,96,8192]{1,0,2:T(2,128)(2,1)} all-to-all(bf16[2,96,8192]{1,0,2:T(2,128)(2,1)} %copy.144), channel_id=1, replica_groups=mesh['dp'=4,'sp'=8] {'sp'}, dimensions={2} | all-to-all | bytes 6291456 | tf_op jit(solution)/shard_map/all_to_all | solution.py:237
  1291.8 11.0 copy.174
  1302.8 6.0 convolution_convert_fusion.4
  1315.9 3.9 copy.153
  1330.3 11.2 reduce-scatter.16.cloned.1.call-done
  1341.5 32.1 %reduce-scatter.18.cloned.1.call-done = bf16[128,256]{1,0:T(8,128)(2,1)} async-done(((bf16[1024,256]{1,0:T(8,128)(2,1)}), bf16[128,256]{1,0:T(8,128)(2,1)}) %reduce-scatter.18.cloned.1.call-update) | async-done | bytes 65552 | tf_op jit(solution)/shard_map/reduce_scatter | solution.py:259
  1373.6 36.8 %reduce-scatter.20.cloned.1.call-done = bf16[128,1024]{1,0:T(8,128)(2,1)} async-done(((bf16[1024,1024]{1,0:T(8,128)(2,1)}), bf16[128,1024]{1,0:T(8,128)(2,1)}) %reduce-scatter.20.cloned.1.call-update) | async-done | bytes 262160 | tf_op jit(solution)/shard_map/reduce_scatter | solution.py:262
  1410.5 11.5 add_convert_fusion
  1425.9 9.1 fusion.70
  1434.9 14.8 all-reduce.2
  1449.8 9.8 all-reduce.3
  1460.6 6.9 fusion.72
  1467.5 5.3 copy.155
  1472.9 23.2 %all-reduce.7.cloned.1.call-done = (bf16[128,256]{1,0:T(8,128)(2,1)}, bf16[128,256]{1,0:T(8,128)(2,1)}, bf16[128,1024]{1,0:T(8,128)(2,1)}, bf16[1024,128]{1,0:T(...) async-done(((bf16[128,256]{1,0:T(8,128)(2,1)}, bf16[128,256]{1,0:T(8,128)(2,1)}, bf16[128,1024]{1,0:T(8,128)(2,1)}, ...) | async-done | bytes 2768912 | tf_op jit(solution)/shard_map/psum | solution.py:283
  (1273 shorter events, 702.2 us)
Async XLA Ops:
  7.2 51.7 %all-gather.8.cloned.1.call-start = ((), (), s32[]{:S(2)}) async-start(), calls=%async_computation.11 | async-start | bytes 2359296 | tf_op jit(solution)/shard_map/all_gather | solution.py:135
  9.0 540.6 %all-gather.10.cloned.1.call-start = ((), (), s32[]{:S(2)}) async-start(), calls=%async_computation.12 | async-start | bytes 2359296 | tf_op jit(solution)/shard_map/all_gather | solution.py:136
  9.8 550.5 %all-gather.14.cloned.1.call-start = ((), (), s32[]{:S(2)}) async-start(), calls=%async_computation.14 | async-start | bytes 6340608 | tf_op jit(solution)/shard_map/all_gather | solution.py:141
  10.5 562.3 %all-gather.12.cloned.1.call-start = ((), (), s32[]{:S(2)}) async-start(), calls=%async_computation.13 | async-start | bytes 6340608 | tf_op jit(solution)/shard_map/all_gather | solution.py:140
  11.1 16.4 %copy-start.22 = (bf16[128,256]{1,0:T(8,128)(2,1)S(1)}, bf16[128,256]{1,0:T(8,128)(2,1)}, u32[]{:S(2)}) copy-start(bf16[128,256]{1,0:T(8,128)(2,1)} %param.19) | copy-start | bytes 196612
  11.1 16.5 %copy-start.23 = (bf16[128,256]{1,0:T(8,128)(2,1)S(1)}, bf16[128,256]{1,0:T(8,128)(2,1)}, u32[]{:S(2)}) copy-start(bf16[128,256]{1,0:T(8,128)(2,1)} %param.20) | copy-start | bytes 196612
  14.0 538.9 %copy-start = (bf16[1024,1024]{0,1:T(8,128)(2,1)}, bf16[1024,1024]{0,1:T(8,128)(2,1)S(1)}, u32[]{:S(2)}) copy-start(bf16[1024,1024]{0,1:T(8,128)(2,1)S(1)} %copy.122) | copy-start | bytes 6291460
  27.5 33.4 %copy-start.27 = (f32[8,1,128]{2,1,0:T(1,128)}, f32[8,1,128]{2,1,0:T(1,128)S(1)}, u32[]{:S(2)}) copy-start(f32[8,1,128]{2,1,0:T(1,128)S(1)} %convert_element_type.246) | copy-start | bytes 12292
  28.8 32.0 %copy-start.29 = (f32[1024]{0:T(1024)}, f32[1024]{0:T(1024)S(1)}, u32[]{:S(2)}) copy-start(f32[1024]{0:T(1024)S(1)} %fusion.80) | copy-start | bytes 12292
  60.9 5.0 copy-start.7
  65.9 5.7 copy-start.26
  65.9 123.0 %all-to-all-start = ((bf16[16,96,1024]{2,1,0:T(8,128)(2,1)}), bf16[16,96,1024]{2,1,0:T(8,128)(2,1)}, u32[]{:S(2)}, u32[]{:S(2)}) async-start(bf16[16,96,1024]{2,1,0:T(8,128)(2,1)} %bitcast.333), calls=%async_computation | async-start | bytes 6291456 | tf_op jit(solution)/shard_map/all_to_all | solution.py:152
  70.5 513.7 %all-gather.16.cloned.1.call-start = ((), (), s32[]{:S(2)}) async-start(), calls=%async_computation.15 | async-start | bytes 6340608 | tf_op jit(solution)/shard_map/all_gather | solution.py:142
  219.2 4.9 copy-start.36
  236.5 4.9 copy-start.36
  253.9 4.8 copy-start.36
  271.3 4.8 copy-start.36
  288.7 4.8 copy-start.36
  306.0 4.8 copy-start.36
  340.8 4.8 copy-start.36
  358.1 4.8 copy-start.36
  375.5 4.8 copy-start.36
  392.8 4.9 copy-start.36
  410.2 4.9 copy-start.36
  427.6 4.9 copy-start.36
  444.9 4.8 copy-start.36
  462.3 4.9 copy-start.36
  479.7 4.8 copy-start.36
  498.2 5.6 copy-start.33
  498.2 54.7 %all-to-all-start.1 = ((bf16[128,8,1024]{2,0,1:T(8,128)(2,1)}), bf16[128,8,1024]{2,0,1:T(8,128)(2,1)}, u32[]{:S(2)}, u32[]{:S(2)}) async-start(bf16[128,8,1024]{2,0,1:T(8,128)(2,1)} %copy.131), calls=%async_computation.1 | async-start | bytes 4194304 | tf_op jit(solution)/shard_map/all_to_all | solution.py:172
  503.8 818.0 %reduce-scatter.22.cloned.1.call-start = ((), (), s32[]{:S(2)}) async-start(), calls=%async_computation.19 | async-start | bytes 2359296
  572.8 11.3 copy-start.9
  604.2 11.5 copy-start.3
  604.2 11.5 copy-start.39
  615.7 10.2 copy-start.5
  638.3 685.3 %reduce-scatter.28.cloned.1.call-start = ((), (), s32[]{:S(2)}) async-start(), calls=%async_computation.22 | async-start | bytes 6488064
  657.5 668.3 %reduce-scatter.24.cloned.1.call-start = ((), (), s32[]{:S(2)}) async-start(), calls=%async_computation.20 | async-start | bytes 6488064
  685.3 93.3 %all-to-all-start.2 = ((bf16[8,128,1024]{2,1,0:T(8,128)(2,1)}), bf16[8,128,1024]{2,1,0:T(8,128)(2,1)S(1)}, u32[]{:S(2)}, u32[]{:S(2)}) async-start(bf16[8,128,1024]{2,1,0:T(8,128)(2,1)} %bitcast.339), calls=%async_computation.2 | async-start | bytes 4194304 | tf_op jit(solution)/shard_map/all_to_all | solution.py:232
  695.5 632.6 %reduce-scatter.26.cloned.1.call-start = ((), (), s32[]{:S(2)}) async-start(), calls=%async_computation.21 | async-start | bytes 6488064
  714.2 627.3 %reduce-scatter.16.cloned.1.call-start = ((), (), s32[]{:S(2)}) async-start(), calls=%async_computation.16 | async-start | bytes 589824 | tf_op jit(solution)/shard_map/reduce_scatter | solution.py:256
  1291.8 11.0 copy-start.1
  1291.8 11.0 copy-start.28
  1291.8 11.0 copy-start.30
  1311.6 62.0 %reduce-scatter.18.cloned.1.call-start = ((), (), s32[]{:S(2)}) async-start(), calls=%async_computation.17 | async-start | bytes 589824 | tf_op jit(solution)/shard_map/reduce_scatter | solution.py:259
  1312.7 97.7 %reduce-scatter.20.cloned.1.call-start = ((), (), s32[]{:S(2)}) async-start(), calls=%async_computation.18 | async-start | bytes 2359296 | tf_op jit(solution)/shard_map/reduce_scatter | solution.py:262
  1319.9 176.2 %all-reduce.7.cloned.1.call-start = ((), (), s32[]{:S(2)}) async-start(), calls=%async_computation.23 | async-start | bytes 5537792 | tf_op jit(solution)/shard_map/psum | solution.py:283
  1425.9 9.1 copy-start.31
  1425.9 34.8 %copy-start.25 = (f32[1024]{0:T(1024)S(1)}, f32[1024]{0:T(1024)}, u32[]{:S(2)}) copy-start(f32[1024]{0:T(1024)} %copy-done.24) | copy-start | bytes 12292
  (113 other events, 213.2 us)
Sparse Core Ops, SparseCore 0:
  10.2 37.7 all-gather.7
  49.5 39.1 all-gather.9
  90.3 103.3 all-gather.13
  195.2 58.0 all-gather.11
  254.8 57.9 all-gather.15
  638.4 42.0 reduce-scatter.21
  682.7 100.5 reduce-scatter.27
  785.6 70.4 reduce-scatter.23
  858.4 63.2 reduce-scatter.25
  1311.8 29.6 reduce-scatter.15
  1344.4 29.1 reduce-scatter.17
  1376.3 34.0 reduce-scatter.19
  1415.0 81.0 all-reduce.6
where the time goes:
time: 1530 us; the launch traced here: 1510 us
  matrix products  473 us (31%)
  waiting for transfers between devices  289 us (19%)
  local copies, waits for them, and re-layouts  286 us (19%)
  blocking collectives  208 us (14%)
  other arithmetic  170 us (11%)
  loops' own time  48 us (3%)
  starting transfers between devices  20.9 us (1%)
  between operations  15.3 us (1%)
    dot_general x64, matrix products, attend_block(): jnp.einsum('hij,hjv->hiv', weights, value_blk, precision=CAREFUL)  118 us
    all_to_all x1, waiting for transfers between devices, body(): lax.all_to_all(projected.reshape(head_count, per_head, tok_local), 'sp',...  116 us
    all_to_all x1, blocking collectives, body(): lax.all_to_all(grad_stack, 'sp', split_axis=2, concat_axis=0, tiled=True)  98.5 us
    unnamed x91, local copies, waits for them, and re-layouts  80.6 us
    dot_general x64, matrix products, attend_block(): scores = jnp.einsum('hif,hjf->hij', query_blk, key_blk, precision=CAREFUL)  75.8 us
    all_to_all x1, waiting for transfers between devices, body(): lax.all_to_all(grad_attended, 'sp', split_axis=0, concat_axis=1, tiled=True)  64.4 us
    squeeze x64, local copies, waits for them, and re-layouts, attend(): lax.scan(jax.checkpoint(attend_block), initial, (blocked(queries), blocke...  56.3 us
    dynamic_slice x48, local copies, waits for them, and re-layouts, attend(): lax.scan(jax.checkpoint(attend_block), initial, (blocked(queries), blocke...  50.9 us
  transfers between devices with their start and end apart: 16, of which 7 were waited for; matrix products, arithmetic and copies ran while one was open for 56% of the time, Pallas kernels for 0%

commit v1 on v0

--- a/solution.py
+++ b/solution.py
@@ -9,6 +9,27 @@
 BLOCK = 512
 EPSILON = 1e-05
 CAREFUL = lax.Precision.HIGH
+
+
+def gather_around(value, axis, dim):
+    devices, mine, rows = (lax.axis_size(axis), lax.axis_index(axis), value.shape[dim])
+    right = [(i, (i + 1) % devices) for i in range(devices)]
+    behind = [(i, (i - 1) % devices) for i in range(devices)]
+    out = jnp.zeros((*value.shape[:dim], devices * rows, *value.shape[dim + 1 :]), value.dtype)
+    out = lax.dynamic_update_slice_in_dim(out, value, mine * rows, axis=dim)
+    from_left = from_right = value
+    half = devices // 2
+    for step in range(1, half + 1):
+        from_left = lax.ppermute(from_left, axis, right)
+        out = lax.dynamic_update_slice_in_dim(
+            out, from_left, (mine - step) % devices * rows, axis=dim
+        )
+        if step < devices - half:
+            from_right = lax.ppermute(from_right, axis, behind)
+            out = lax.dynamic_update_slice_in_dim(
+                out, from_right, (mine + step) % devices * rows, axis=dim
+            )
+    return out
 
 
 def rms_scale(values, weights):
@@ -136,7 +157,7 @@
         lax.all_gather(w_out, "sp", axis=1, tiled=True),
     )
     mlp_full = (
-        lax.all_gather(gain_mlp, "sp", axis=0, tiled=True),
+        gather_around(gain_mlp, "sp", 0),
         lax.all_gather(w_gate, "sp", axis=0, tiled=True),
         lax.all_gather(w_up, "sp", axis=0, tiled=True),
         lax.all_gather(w_down, "sp", axis=1, tiled=True),

time: 1530 us -> 1510 us (0.987)
  blocking collectives: 208 us -> 167 us
  waiting for transfers between devices: 289 us -> 310 us
    all_gather x1 -> x0, blocking collectives: 41.4 us -> none  [body(): lax.all_gather(gain_mlp, 'sp', axis=0, tiled=True)]
    ppermute x0 -> x7, waiting for transfers between devices: none -> 34.7 us  [the longest x4 34.7 us: gather_around(): from_left = lax.ppermute(from_left, axis, right)]
  transfers between devices with their start and end apart: 16 -> 23, of which waited for: 7 -> 10; matrix products, arithmetic and copies ran while one was open for 56% -> 57% of each run, Pallas kernels for 0% -> 0%
where the time goes in v1:
time: 1510 us; the launch traced here: 1500 us
  matrix products  472 us (31%)
  waiting for transfers between devices  310 us (21%)
  local copies, waits for them, and re-layouts  286 us (19%)
  other arithmetic  170 us (11%)
  blocking collectives  167 us (11%)
  loops' own time  47.7 us (3%)
  starting transfers between devices  29.2 us (2%)
  between operations  15.3 us (1%)
    dot_general x64, matrix products, attend_block(): jnp.einsum('hij,hjv->hiv', weights, value_blk, precision=CAREFUL)  118 us
    all_to_all x1, waiting for transfers between devices, body(): lax.all_to_all(projected.reshape(head_count, per_head, tok_local), 'sp',...  106 us
    all_to_all x1, blocking collectives, body(): lax.all_to_all(grad_stack, 'sp', split_axis=2, concat_axis=0, tiled=True)  98.5 us
    unnamed x91, local copies, waits for them, and re-layouts  79.4 us
    dot_general x64, matrix products, attend_block(): scores = jnp.einsum('hif,hjf->hij', query_blk, key_blk, precision=CAREFUL)  75.9 us
    all_to_all x1, waiting for transfers between devices, body(): lax.all_to_all(grad_attended, 'sp', split_axis=0, concat_axis=1, tiled=True)  63.8 us
    squeeze x64, local copies, waits for them, and re-layouts, attend(): lax.scan(jax.checkpoint(attend_block), initial, (blocked(queries), blocke...  56.3 us
    dynamic_slice x48, local copies, waits for them, and re-layouts, attend(): lax.scan(jax.checkpoint(attend_block), initial, (blocked(queries), blocke...  51.4 us
  transfers between devices with their start and end apart: 23, of which 10 were waited for; matrix products, arithmetic and copies ran while one was open for 57% of the time, Pallas kernels for 0%

profile of v1, /device:TPU:0, one launch (start us, length us, event | category | flops | bytes accessed | tf_op | source)
XLA Modules:
  0.0 1496.8 jit_solution(7760946045770398091)
XLA Ops:
  14.1 13.4 all-gather
  28.8 16.1 %all_gather.31 = bf16[1024,256]{0,1:T(8,128)(2,1)S(1)} all-gather(bf16[128,256]{0,1:T(8,128)(2,1)S(1)} %copy.123), channel_id=1, replica_groups=mesh['dp'=4,'sp'=8] {'sp'}, dimensions={0}, use_global_device_ids=true | all-gather | bytes 589824 | tf_op jit(solution)/shard_map/all_gather | solution.py:154
  45.0 13.9 all_gather.32
  60.9 5.0 convolution_convert_fusion.3
  65.9 4.6 all-to-all-start
  73.0 106.1 %all-to-all-done = bf16[16,96,1024]{2,1,0:T(8,128)(2,1)} async-done(((bf16[16,96,1024]{2,1,0:T(8,128)(2,1)}), bf16[16,96,1024]{2,1,0:T(8,128)(2,1)}, u32[]{:S(2)}, u32[]{:S(2)}) %all-to-all-start) | async-done | bytes 3145760 | tf_op jit(solution)/shard_map/all_to_all | solution.py:173
  192.0 4.4 copy.128
  198.0 276.6 %while.47 = (s32[]{:T(128)}, f32[2,273,64]{1,2,0:T(8,128)S(1)}, f32[2,273]{1,0:T(2,128)S(1)}, s32[]{:T(128)}, bf16[16,2,512,64]{2,3,1,0:T(8,128)(2,1)}, /*index=...) while((s32[]{:T(128)}, f32[2,273,64]{1,2,0:T(8,128)S(1)}, ...), condition=%wide.region_4.5_spmd.clone, body=%wide.region_1.4_spmd.clone.sunk | while | flops 477021408 | bytes 14363353 | solution.py:105
  474.6 4.2 copy.130
  478.7 4.1 convert_element_type.212
  482.8 4.1 copy.131
  486.9 4.5 all-to-all-start.1
  499.1 30.5 %collective-permute-done = bf16[128]{0:T(256)(128)(2,1)S(1)} collective-permute-done((bf16[128]{0:T(256)(128)(2,1)S(1)}, bf16[128]{0:T(256)(128)(2,1)S(1)}, u32[]{:S(2)}, u32[]{:S(2)}) %collective-permute-start) | collective-permute-done | bytes 288 | tf_op jit(solution)/shard_map/ppermute | solution.py:23
  544.1 11.2 fusion.87
  555.3 4.8 multiply_reduce_fusion.6
  562.6 12.0 fusion.89
  574.6 20.4 %multiply_convert_fusion = (bf16[1024,2752]{0,1:T(8,128)(2,1)}, bf16[1024,2752]{0,1:T(8,128)(2,1)}, bf16[1024,2752]{0,1:T(8,128)(2,1)}) fusion(f32[1024,2752]{0,1:T(8,128)} %fusion.87, f32[1024,2752]{0,1:T(8,128)} %fusion.89, bf16[1024,2752]{0,1:T(8,128)(2,1)} %all-gather.11.cloned.1.call-done, bf16[1024,1024]{0,1:T(8,128)(2,1)S(1)} %multiply_convert_fusion.3), kind=kOutput, calls=%fused_computation.130 | convolution fusion | flops 5816451072 | bytes 47185920 | tf_op jit(solution)/shard_map/dot_general | solution.py:200
  595.0 11.3 fusion.88
  606.3 10.3 multiply_reduce_fusion.4
  619.7 4.0 convolution_convert_fusion.6
  628.2 10.4 convolution_convert_fusion
  638.6 8.3 copy.183
  648.5 10.5 convolution_convert_fusion.1
  659.0 8.3 copy.181
  669.0 5.8 convolution_convert_fusion.5
  674.8 7.3 all-to-all-start.2
  682.2 10.3 convolution_convert_fusion.2
  692.5 8.3 copy.179
  700.9 63.8 %all-to-all-done.2 = bf16[8,128,1024]{2,1,0:T(8,128)(2,1)S(1)} async-done(((bf16[8,128,1024]{2,1,0:T(8,128)(2,1)}), bf16[8,128,1024]{2,1,0:T(8,128)(2,1)S(1)}, u32[]{:S(2)}, u32[]{:S(2)}) %all-to-all-start.2) | async-done | bytes 2097184 | tf_op jit(solution)/shard_map/all_to_all | solution.py:253
  765.2 4.4 copy.136
  769.6 5.0 reshape.355
  776.3 394.1 %while.48 = (s32[]{:T(128)}, f32[2,273,64]{1,2,0:T(8,128)S(1)}, f32[2,273]{1,0:T(2,128)S(1)}, bf16[16,2,512,16]{2,3,1,0:T(8,128)(2,1)S(1)}, bf16[16,2,512,16]{2,...) while((s32[]{:T(128)}, f32[2,273,64]{1,2,0:T(8,128)S(1)}, ...), condition=%wide.region_14.15_spmd.clone, body=%wide.region_7.14_spmd.clone.sunk | while | flops 1318872064 | bytes 42693776 | solution.py:105
  1172.4 7.0 copy.144
  1179.4 98.5 %all_to_all.53 = bf16[2,96,8192]{1,0,2:T(2,128)(2,1)} all-to-all(bf16[2,96,8192]{1,0,2:T(2,128)(2,1)} %copy.144), channel_id=1, replica_groups=mesh['dp'=4,'sp'=8] {'sp'}, dimensions={2} | all-to-all | bytes 6291456 | tf_op jit(solution)/shard_map/all_to_all | solution.py:258
  1277.9 11.0 copy.174
  1289.0 6.0 convolution_convert_fusion.4
  1302.0 3.9 copy.153
  1316.4 11.2 reduce-scatter.16.cloned.1.call-done
  1327.7 32.1 %reduce-scatter.18.cloned.1.call-done = bf16[128,256]{1,0:T(8,128)(2,1)} async-done(((bf16[1024,256]{1,0:T(8,128)(2,1)}), bf16[128,256]{1,0:T(8,128)(2,1)}) %reduce-scatter.18.cloned.1.call-update) | async-done | bytes 65552 | tf_op jit(solution)/shard_map/reduce_scatter | solution.py:280
  1359.8 36.8 %reduce-scatter.20.cloned.1.call-done = bf16[128,1024]{1,0:T(8,128)(2,1)} async-done(((bf16[1024,1024]{1,0:T(8,128)(2,1)}), bf16[128,1024]{1,0:T(8,128)(2,1)}) %reduce-scatter.20.cloned.1.call-update) | async-done | bytes 262160 | tf_op jit(solution)/shard_map/reduce_scatter | solution.py:283
  1396.6 11.5 add_convert_fusion
  1408.1 3.9 copy.154
  1412.0 9.1 fusion.70
  1421.1 14.7 all-reduce.2
  1436.0 9.8 all-reduce.3
  1446.8 6.9 fusion.72
  1453.8 5.3 copy.155
  1459.1 23.1 %all-reduce.7.cloned.1.call-done = (bf16[128,256]{1,0:T(8,128)(2,1)}, bf16[128,256]{1,0:T(8,128)(2,1)}, bf16[128,1024]{1,0:T(8,128)(2,1)}, bf16[1024,128]{1,0:T(...) async-done(((bf16[128,256]{1,0:T(8,128)(2,1)}, bf16[128,256]{1,0:T(8,128)(2,1)}, bf16[128,1024]{1,0:T(8,128)(2,1)}, ...) | async-done | bytes 2768912 | tf_op jit(solution)/shard_map/psum | solution.py:304
  (1295 shorter events, 715.2 us)
Async XLA Ops:
  7.2 51.8 %all-gather.7.cloned.1.call-start = ((), (), s32[]{:S(2)}) async-start(), calls=%async_computation.11 | async-start | bytes 2359296 | tf_op jit(solution)/shard_map/all_gather | solution.py:156
  9.0 535.1 %all-gather.15.cloned.1.call-start = ((), (), s32[]{:S(2)}) async-start(), calls=%async_computation.15 | async-start | bytes 6340608 | tf_op jit(solution)/shard_map/all_gather | solution.py:163
  9.8 545.5 %all-gather.9.cloned.1.call-start = ((), (), s32[]{:S(2)}) async-start(), calls=%async_computation.12 | async-start | bytes 2359296 | tf_op jit(solution)/shard_map/all_gather | solution.py:157
  10.5 552.0 %all-gather.13.cloned.1.call-start = ((), (), s32[]{:S(2)}) async-start(), calls=%async_computation.14 | async-start | bytes 6340608 | tf_op jit(solution)/shard_map/all_gather | solution.py:162
  11.1 16.4 %copy-start.22 = (bf16[128,256]{1,0:T(8,128)(2,1)S(1)}, bf16[128,256]{1,0:T(8,128)(2,1)}, u32[]{:S(2)}) copy-start(bf16[128,256]{1,0:T(8,128)(2,1)} %param.19) | copy-start | bytes 196612
  11.1 16.5 %copy-start.23 = (bf16[128,256]{1,0:T(8,128)(2,1)S(1)}, bf16[128,256]{1,0:T(8,128)(2,1)}, u32[]{:S(2)}) copy-start(bf16[128,256]{1,0:T(8,128)(2,1)} %param.20) | copy-start | bytes 196612
  14.0 541.3 %copy-start = (bf16[1024,1024]{0,1:T(8,128)(2,1)}, bf16[1024,1024]{0,1:T(8,128)(2,1)S(1)}, u32[]{:S(2)}) copy-start(bf16[1024,1024]{0,1:T(8,128)(2,1)S(1)} %copy.122) | copy-start | bytes 6291460
  27.5 33.4 %copy-start.27 = (f32[8,1,128]{2,1,0:T(1,128)}, f32[8,1,128]{2,1,0:T(1,128)S(1)}, u32[]{:S(2)}) copy-start(f32[8,1,128]{2,1,0:T(1,128)S(1)} %convert_element_type.246) | copy-start | bytes 12292
  28.8 32.1 %copy-start.29 = (f32[1024]{0:T(1024)}, f32[1024]{0:T(1024)S(1)}, u32[]{:S(2)}) copy-start(f32[1024]{0:T(1024)S(1)} %fusion.80) | copy-start | bytes 12292
  60.9 5.0 copy-start.7
  65.9 5.7 copy-start.26
  65.9 113.2 %all-to-all-start = ((bf16[16,96,1024]{2,1,0:T(8,128)(2,1)}), bf16[16,96,1024]{2,1,0:T(8,128)(2,1)}, u32[]{:S(2)}, u32[]{:S(2)}) async-start(bf16[16,96,1024]{2,1,0:T(8,128)(2,1)} %bitcast.331), calls=%async_computation | async-start | bytes 6291456 | tf_op jit(solution)/shard_map/all_to_all | solution.py:173
  70.5 504.1 %all-gather.11.cloned.1.call-start = ((), (), s32[]{:S(2)}) async-start(), calls=%async_computation.13 | async-start | bytes 6340608 | tf_op jit(solution)/shard_map/all_gather | solution.py:161
  209.3 4.9 copy-start.37
  226.6 4.9 copy-start.37
  243.9 4.9 copy-start.37
  261.2 4.8 copy-start.37
  278.4 4.9 copy-start.37
  330.3 4.8 copy-start.37
  364.8 4.9 copy-start.37
  399.4 4.9 copy-start.37
  433.9 4.9 copy-start.37
  486.9 68.4 %all-to-all-start.1 = ((bf16[128,8,1024]{2,0,1:T(8,128)(2,1)}), bf16[128,8,1024]{2,0,1:T(8,128)(2,1)}, u32[]{:S(2)}, u32[]{:S(2)}) async-start(bf16[128,8,1024]{2,0,1:T(8,128)(2,1)} %copy.131), calls=%async_computation.1 | async-start | bytes 4194304 | tf_op jit(solution)/shard_map/all_to_all | solution.py:193
  491.3 816.5 %reduce-scatter.22.cloned.1.call-start = ((), (), s32[]{:S(2)}) async-start(), calls=%async_computation.19 | async-start | bytes 2359296
  491.4 38.2 %collective-permute-start = (bf16[128]{0:T(256)(128)(2,1)S(1)}, bf16[128]{0:T(256)(128)(2,1)S(1)}, u32[]{:S(2)}, u32[]{:S(2)}) collective-permute-start(bf16[128]{0:T(256)(128)(2,1)S(1)} %copy-done.35), channel_id=1, source_target_pairs={{0,1},{1,2},{2,3},{3,4},{4,5},{5,6},{6,7},{7,0},{8,9},{9,10},{10,1... | collective-permute-start | bytes 776 | tf_op jit(solution)/shard_map/ppermute | solution.py:23
  491.8 37.8 %collective-permute-start.1 = (bf16[128]{0:T(256)(128)(2,1)S(1)}, bf16[128]{0:T(256)(128)(2,1)S(1)}, u32[]{:S(2)}, u32[]{:S(2)}) collective-permute-start(bf16[128]{0:T(256)(128)(2,1)S(1)} %copy-done.35), channel_id=1, source_target_pairs={{0,7},{1,0},{2,1},{3,2},{4,3},{5,4},{6,5},{7,6},{8,15},{9,8},{10,9... | collective-permute-start | bytes 776 | tf_op jit(solution)/shard_map/ppermute | solution.py:28
  529.6 4.8 collective-permute-start.2
  529.6 5.1 collective-permute-start.3
  534.4 4.8 collective-permute-start.4
  534.8 6.8 collective-permute-start.5
  539.2 4.8 collective-permute-start.6
  562.5 12.1 copy-start.10
  595.0 11.3 copy-start.3
  595.0 11.3 copy-start.33
  606.3 10.3 copy-start.5
  626.7 683.0 %reduce-scatter.28.cloned.1.call-start = ((), (), s32[]{:S(2)}) async-start(), calls=%async_computation.22 | async-start | bytes 6488064
  647.0 665.0 %reduce-scatter.26.cloned.1.call-start = ((), (), s32[]{:S(2)}) async-start(), calls=%async_computation.21 | async-start | bytes 6488064
  674.8 89.9 %all-to-all-start.2 = ((bf16[8,128,1024]{2,1,0:T(8,128)(2,1)}), bf16[8,128,1024]{2,1,0:T(8,128)(2,1)S(1)}, u32[]{:S(2)}, u32[]{:S(2)}) async-start(bf16[8,128,1024]{2,1,0:T(8,128)(2,1)} %bitcast.337), calls=%async_computation.2 | async-start | bytes 4194304 | tf_op jit(solution)/shard_map/all_to_all | solution.py:253
  682.1 632.0 %reduce-scatter.24.cloned.1.call-start = ((), (), s32[]{:S(2)}) async-start(), calls=%async_computation.20 | async-start | bytes 6488064
  700.9 626.8 %reduce-scatter.16.cloned.1.call-start = ((), (), s32[]{:S(2)}) async-start(), calls=%async_computation.16 | async-start | bytes 589824 | tf_op jit(solution)/shard_map/reduce_scatter | solution.py:277
  1277.9 11.1 copy-start.1
  1277.9 11.1 copy-start.28
  1277.9 11.1 copy-start.30
  1297.8 62.0 %reduce-scatter.18.cloned.1.call-start = ((), (), s32[]{:S(2)}) async-start(), calls=%async_computation.17 | async-start | bytes 589824 | tf_op jit(solution)/shard_map/reduce_scatter | solution.py:280
  1298.8 97.8 %reduce-scatter.20.cloned.1.call-start = ((), (), s32[]{:S(2)}) async-start(), calls=%async_computation.18 | async-start | bytes 2359296 | tf_op jit(solution)/shard_map/reduce_scatter | solution.py:283
  1306.0 176.2 %all-reduce.7.cloned.1.call-start = ((), (), s32[]{:S(2)}) async-start(), calls=%async_computation.23 | async-start | bytes 5537792 | tf_op jit(solution)/shard_map/psum | solution.py:304
  1412.0 9.1 copy-start.31
  1412.0 34.8 %copy-start.25 = (f32[1024]{0:T(1024)S(1)}, f32[1024]{0:T(1024)}, u32[]{:S(2)}) copy-start(f32[1024]{0:T(1024)} %copy-done.24) | copy-start | bytes 12292
  (120 other events, 245.8 us)
Sparse Core Ops, SparseCore 0:
  10.2 37.7 all-gather.6
  49.5 112.0 all-gather.14
  163.2 29.9 all-gather.8
  194.6 62.4 all-gather.12
  258.5 59.5 all-gather.10
  626.8 38.9 reduce-scatter.21
  668.1 99.4 reduce-scatter.27
  769.8 71.8 reduce-scatter.25
  844.0 63.1 reduce-scatter.23
  1297.9 29.7 reduce-scatter.15
  1330.6 29.1 reduce-scatter.17
  1362.5 34.0 reduce-scatter.19
  1401.1 81.0 all-reduce.6
